TPU v7x, 32 devices: a whole 2x2x4 slice. The times are simulated.
32 devices in a mesh: section: 4 (over y, x), sta: 8 (over z, core).
Axes of the slice: x: 2, y: 2, z: 4, core: 2. Of those that a mesh axis runs over, the one named last changes fastest.
Arguments:
- waveforms: bfloat16 [4, 64, 8, 4096], P('section', 'sta'), may hold values from -6 to 6
- segment_mask: int32 [4, 64, 8], P('section', 'sta'), may hold values 0 or 1
- pair_blocks: int32 [8, 4], P('sta'), may hold values from 0 to 7, as said below
- window_decay: float32 [4], P('section'), may hold values from 0.5 to 1
Outputs:
- stacked: bfloat16 [4, 64, 32, 384], P('section', 'sta')
Inputs may be any that keep to these rules, and one draw needn't show every extreme that they name: `pair_blocks`: entry k of row b names a block of 8 stations other than b; entries of a row may repeat.
All inputs are finite; a program needn't handle non-finite values. No bound on the sum of `segment_mask` on one device may be relied on, other than what follows from the above.
Results may differ from a plain program's by a relative error of at most 0.008.
Values may be sent and summed in bfloat16 or wider, within the bound.
A program may use at most 64 MiB of HBM per device.

v0:
```python
import functools
import math

import jax
import jax.numpy as jnp
import numpy as np
from jax import lax
from jax.experimental import pallas as pl
from jax.experimental.pallas import tpu as pltpu
from jax.sharding import PartitionSpec as P

MESH = pl.DeviceIdType.MESH
RADIX = 64
NF = 1024
LAGS = 384
SMOOTH_HALF = 32
LANES = 128
SUB = 8
EPSILON = 1e-05
NSAMP = RADIX * RADIX
FIRST = NSAMP // LANES
SLICES = FIRST // SUB
BINS = NF // FIRST


def dft_tables():
    b = np.arange(LANES)
    m = np.arange(BINS)
    phi = 2.0 * np.pi * ((b[:, None] * (m[None, :] + 2 * RADIX // FIRST)) % LANES) / LANES
    table = np.zeros((SLICES, 2, LANES, 2, BINS, SLICES))
    for q in range(SLICES):
        table[q, 0, :, 0, :, q] = np.cos(phi)
        table[q, 1, :, 0, :, q] = np.sin(phi)
        table[q, 0, :, 1, :, q] = -np.sin(phi)
        table[q, 1, :, 1, :, q] = np.cos(phi)
    table = (table / RADIX).reshape(SLICES * 2 * LANES, 2 * BINS * SLICES).astype(np.float32)
    high = table.astype(jnp.bfloat16)
    low = (table - high.astype(np.float32)).astype(jnp.bfloat16)
    turn = 2.0 * np.pi * np.arange(FIRST)[:, None] * b[None, :] / NSAMP
    twist = np.stack([np.cos(turn), np.sin(turn)], axis=1).astype(np.float32)
    return high, low, twist


def lag_table():
    f = SUB * np.arange(NF // SUB)[None, :] + np.arange(SUB)[:, None]
    shift = np.arange(LAGS) + NSAMP - LAGS // 2
    theta = 2.0 * np.pi * (((2 * RADIX + f)[:, :, None] * shift) % NSAMP) / NSAMP
    table = np.concatenate([np.cos(theta), -np.sin(theta)], axis=1) / math.sqrt(NF)
    return table.astype(np.float32).astype(jnp.bfloat16)


def real_dft(values):
    size = len(values)
    if size == 1:
        return [(values[0], None)]
    if size == 2:
        return [(values[0] + values[1], None), (values[0] - values[1], None)]
    even, odd = real_dft(values[0::2]), real_dft(values[1::2])
    half = size // 2
    out = [None] * (half + 1)
    for k in range(half // 2 + 1):
        er, ei = even[k]
        pr, pi = odd[k]
        if k == 0:
            out[0] = (er + pr, None)
            out[half] = (er - pr, None)
            continue
        if k * 4 == size:
            out[k] = (er, -pr)
            continue
        c, s = math.cos(2 * math.pi * k / size), math.sin(2 * math.pi * k / size)
        tr, ti = pr * c + pi * s, pi * c - pr * s
        out[k] = (er + tr, ei + ti)
        out[half - k] = (er - tr, ti - ei)
    return out


def spectrum_kernel(stations, x_ref, mask_ref, row_ref, high_ref, low_ref, twist_ref, out_ref, y_ref, z_ref, w_ref):
    rows = stations * SUB

    def first(st, _):
        pieces = [x_ref[0, st, :, a * LANES:(a + 1) * LANES].astype(jnp.float32) for a in range(FIRST)]
        spread = real_dft(pieces)
        base = pl.multiple_of(st * SUB, SUB)
        for k1 in range(FIRST):
            re, im = spread[k1] if 2 * k1 <= FIRST else spread[FIRST - k1]
            c, s = twist_ref[k1, 0:1, :], twist_ref[k1, 1:2, :]
            if im is None:
                yr, yi = re * c, -(re * s)
            elif 2 * k1 <= FIRST:
                yr, yi = re * c + im * s, im * c - re * s
            else:
                yr, yi = re * c - im * s, -(im * c) - re * s
            q, p = k1 // SUB, k1 % SUB
            y_ref[pl.ds(p * rows + base, SUB), 2 * q * LANES:(2 * q + 1) * LANES] = yr
            y_ref[pl.ds(p * rows + base, SUB), (2 * q + 1) * LANES:(2 * q + 2) * LANES] = yi
        return 0

    lax.fori_loop(0, stations, first, 0)
    y = y_ref[...]
    yh = y.astype(jnp.bfloat16)
    yl = (y - yh.astype(jnp.float32)).astype(jnp.bfloat16)
    dot = functools.partial(jnp.dot, preferred_element_type=jnp.float32)
    z_ref[...] = dot(yh, high_ref[...]) + dot(yl, high_ref[...]) + dot(yh, low_ref[...])
    reach = SMOOTH_HALF // SUB

    def second(st, _):
        base = pl.multiple_of(st * SUB, SUB)
        lane = lax.broadcasted_iota(jnp.int32, (SUB, LANES), 1)

        def moved(v, d):
            inside = (lane + d >= 0) & (lane + d < LANES)
            return jnp.where(inside, pltpu.roll(v, (-d) % LANES, 1), 0.0)

        re = [z_ref[pl.ds(p * rows + base, SUB), 0:LANES] for p in range(SUB)]
        im = [z_ref[pl.ds(p * rows + base, SUB), LANES:2 * LANES] for p in range(SUB)]
        amp = [jnp.sqrt(re[p] * re[p] + im[p] * im[p]) for p in range(SUB)]
        pre = [amp[0]]
        for p in range(1, SUB):
            pre.append(pre[-1] + amp[p])
        suf = [amp[SUB - 1]]
        for p in range(SUB - 2, -1, -1):
            suf.insert(0, suf[0] + amp[p])
        middle = pre[-1]
        for d in range(1, reach):
            middle = middle + moved(pre[-1], d) + moved(pre[-1], -d)
        marks = mask_ref[st]
        for p in range(SUB):
            smooth = (middle + moved(suf[p], -reach) + moved(pre[p], reach)) / (2 * SMOOTH_HALF + 1)
            scale = marks / (smooth + EPSILON)
            w_ref[pl.ds(p, SUB, stride=2 * SUB), :] = re[p] * scale
            w_ref[pl.ds(SUB + p, SUB, stride=2 * SUB), :] = im[p] * scale
        out_ref[pl.ds(base, SUB)] = w_ref[...].reshape(SUB, 2 * SUB, LANES).astype(jnp.bfloat16)
        return 0

    lax.fori_loop(0, stations, second, 0)
    out_ref[rows] = row_ref[...]


def gather_kernel(n, own_ref, all_ref, send_sem, recv_sem, cross_send, cross_recv):
    me = lax.axis_index("sta")
    ring = n // 2
    core, place = lax.rem(me, 2), me // 2
    right = lax.rem(place + 1, ring) * 2 + core
    left = lax.rem(place + ring - 1, ring) * 2 + core
    mate = place * 2 + 1 - core
    barrier = pltpu.get_barrier_semaphore()
    peers = [mate, right, left]
    for peer in peers:
        pl.semaphore_signal(barrier, inc=1, device_id={"sta": peer}, device_id_type=MESH)
    pl.semaphore_wait(barrier, len(peers))
    count = own_ref.shape[0]
    cut = count // 2

    def block(step):
        return lax.rem(place + step + 2 * ring, ring) * 2 + core

    def remote(src, dst, i, sems, peer):
        return pltpu.make_async_remote_copy(
            src_ref=src, dst_ref=dst, send_sem=sems[0].at[i], recv_sem=sems[1].at[i],
            device_id={"sta": peer}, device_id_type=MESH,
        )

    rail, inner = (send_sem, recv_sem), (cross_send, cross_recv)
    started = []

    def go(src, dst, i, sems, peer):
        copy = remote(src, dst, i, sems, peer)
        copy.start()
        started.append(copy)
        return copy

    to_right = go(own_ref, all_ref.at[me], 0, rail, right)
    to_left = go(own_ref, all_ref.at[me], 1, rail, left)
    inward = [go(own_ref, all_ref.at[me], 0, inner, mate)]
    slot = 1
    half = ring // 2
    for distance in range(1, half + 1):
        from_left, from_right = block(-distance), block(distance)
        to_right.wait_recv()
        if distance < half:
            to_left.wait_recv()
            if distance + 1 < half:
                to_right = go(all_ref.at[from_left], all_ref.at[from_left], 2 * distance, rail, right)
                to_left = go(all_ref.at[from_right], all_ref.at[from_right], 2 * distance + 1, rail, left)
            else:
                first = pl.ds(0, cut)
                rest = pl.ds(cut, count - cut)
                to_right = go(all_ref.at[from_left, first], all_ref.at[from_left, first], 2 * distance, rail, right)
                to_left = go(all_ref.at[from_right, rest], all_ref.at[from_right, rest], 2 * distance + 1, rail, left)
            inward.append(go(all_ref.at[from_left], all_ref.at[from_left], slot, inner, mate))
            inward.append(go(all_ref.at[from_right], all_ref.at[from_right], slot + 1, inner, mate))
            slot += 2
        else:
            if half > 1:
                to_left.wait_recv()
            else:
                to_left.wait_recv()
            inward.append(go(all_ref.at[from_left], all_ref.at[from_left], slot, inner, mate))
    for copy in inward:
        copy.wait_recv()
    for copy in started:
        copy.wait_send()


def cross_kernel(stations, slots, pair_ref, own_ref, all_ref, table_ref, lag_ref, send_ref, loc_ref, cr_ref, ci_ref):
    segments = SUB
    total = stations * slots * stations
    loc_ref[...] = own_ref[0:stations * segments].astype(jnp.float32)

    def pair(kj, _):
        k, j = kj // stations, lax.rem(kj, stations)
        block = pair_ref[0, k]
        other = [all_ref[block, j * segments + s].astype(jnp.float32) for s in range(segments)]
        for i in range(stations):
            re = im = None
            for s in range(segments):
                ar, ai = loc_ref[i * segments + s, 0:SUB, :], loc_ref[i * segments + s, SUB:2 * SUB, :]
                br, bi = other[s][0:SUB], other[s][SUB:2 * SUB]
                tr, ti = ar * br + ai * bi, ar * bi - ai * br
                re, im = (tr, ti) if re is None else (re + tr, im + ti)
            at = pl.ds(pl.multiple_of((i * slots * stations + kj) * SUB, SUB), SUB)
            cr_ref[at, :] = re
            ci_ref[at, :] = im
        return 0

    lax.fori_loop(0, slots * stations, pair, 0)
    acc = None
    for p in range(SUB):
        at = pl.ds(p, total, stride=SUB)
        lhs = jnp.concatenate([cr_ref[at, :], ci_ref[at, :]], axis=1).astype(jnp.bfloat16)
        term = jnp.dot(lhs, table_ref[p], preferred_element_type=jnp.float32)
        acc = term if acc is None else acc + term
    mine = own_ref[stations * segments].astype(jnp.float32)
    for k in range(slots):
        theirs = all_ref[pair_ref[0, k], stations * segments].astype(jnp.float32)[0:stations]
        for i in range(stations):
            count = jnp.sum(mine[i:i + 1] * theirs, axis=1, keepdims=True)
            at = (i * slots + k) * stations
            value = acc[at:at + stations] / jnp.maximum(count, 1.0)
            lag_ref[at:at + stations, :] = value
    send_ref[...] = lag_ref[...].astype(jnp.bfloat16)


def stack_kernel(windows, lag_ref, send_ref, decay_ref, out_ref, got_ref, rate_ref, acc_ref, send_sem, recv_sem, rate_send, rate_recv):
    me = lax.axis_index("section")
    barrier = pltpu.get_barrier_semaphore()
    for d in range(1, windows):
        pl.semaphore_signal(barrier, inc=1, device_id={"section": lax.rem(me + d, windows)}, device_id_type=MESH)
    pl.semaphore_wait(barrier, windows - 1)

    def copies(source, target):
        peer = {"section": target}
        return (
            pltpu.make_async_remote_copy(
                src_ref=send_ref, dst_ref=got_ref.at[source], send_sem=send_sem.at[target],
                recv_sem=recv_sem.at[source], device_id=peer, device_id_type=MESH),
            pltpu.make_async_remote_copy(
                src_ref=decay_ref, dst_ref=rate_ref.at[source], send_sem=rate_send.at[target],
                recv_sem=rate_recv.at[source], device_id=peer, device_id_type=MESH),
        )

    for d in range(1, windows):
        @pl.when(me + d < windows)
        def _():
            for copy in copies(me, me + d):
                copy.start()
    acc_ref[...] = jnp.zeros_like(acc_ref)
    for v in range(windows - 1):
        @pl.when(v < me)
        def _():
            for copy in copies(v, me):
                copy.wait_recv()
            acc_ref[...] = acc_ref[...] * rate_ref[v, 0:1, 0:1] + got_ref[v].astype(jnp.float32)
    out_ref[...] = (acc_ref[...] * decay_ref[0:1, 0:1] + lag_ref[...]).astype(jnp.bfloat16)
    for d in range(1, windows):
        @pl.when(me + d < windows)
        def _():
            for copy in copies(me, me + d):
                copy.wait_send()


def body(sizes, waveforms, segment_mask, pair_blocks, window_decay):
    n, windows = sizes
    stations, segments = waveforms.shape[1], waveforms.shape[2]
    slots = pair_blocks.shape[1]
    rows = stations * segments
    marks = segment_mask[0].astype(jnp.float32)
    marks_wide = jnp.broadcast_to(marks[:, :, None], (stations, segments, LANES))
    marks_row = jnp.pad(marks, ((0, 2 * SUB - stations), (0, LANES - segments))).astype(jnp.bfloat16)
    high, low, twist = dft_tables()
    vmem = pl.BlockSpec(memory_space=pltpu.VMEM)
    smem = pl.BlockSpec(memory_space=pltpu.SMEM)
    tile = (rows + 1, 2 * SUB, LANES)
    own = pl.pallas_call(
        functools.partial(spectrum_kernel, stations),
        name="spectrum",
        out_shape=jax.ShapeDtypeStruct(tile, jnp.bfloat16),
        in_specs=[vmem] * 6,
        out_specs=vmem,
        scratch_shapes=[
            pltpu.VMEM((SUB * rows, SLICES * 2 * LANES), jnp.float32),
            pltpu.VMEM((SUB * rows, 2 * LANES), jnp.float32),
            pltpu.VMEM((SUB * 2 * SUB, LANES), jnp.float32),
        ],
    )(waveforms, marks_wide, marks_row, jnp.asarray(high), jnp.asarray(low), jnp.asarray(twist))
    dma = pltpu.SemaphoreType.DMA
    gathered = pl.pallas_call(
        functools.partial(gather_kernel, n),
        name="gather",
        out_shape=jax.ShapeDtypeStruct((n,) + tile, jnp.bfloat16),
        in_specs=[vmem],
        out_specs=vmem,
        scratch_shapes=[dma((n,)), dma((n,)), dma((n,)), dma((n,))],
        compiler_params=pltpu.CompilerParams(collective_id=0, has_side_effects=True),
    )(own)
    total = stations * slots * stations
    lagged, sent = pl.pallas_call(
        functools.partial(cross_kernel, stations, slots),
        name="cross",
        out_shape=(
            jax.ShapeDtypeStruct((total, LAGS), jnp.float32),
            jax.ShapeDtypeStruct((total, LAGS), jnp.bfloat16),
        ),
        in_specs=[smem, vmem, vmem, vmem],
        out_specs=(vmem, vmem),
        scratch_shapes=[
            pltpu.VMEM((rows, 2 * SUB, LANES), jnp.float32),
            pltpu.VMEM((total * SUB, LANES), jnp.float32),
            pltpu.VMEM((total * SUB, LANES), jnp.float32),
        ],
    )(pair_blocks, own, gathered, jnp.asarray(lag_table()))
    decay = jnp.broadcast_to(window_decay[:, None], (SUB, LANES))
    stacked = pl.pallas_call(
        functools.partial(stack_kernel, windows),
        name="stack",
        out_shape=jax.ShapeDtypeStruct((total, LAGS), jnp.bfloat16),
        in_specs=[vmem] * 3,
        out_specs=vmem,
        scratch_shapes=[
            pltpu.VMEM((windows, total, LAGS), jnp.bfloat16),
            pltpu.VMEM((windows, SUB, LANES), jnp.float32),
            pltpu.VMEM((total, LAGS), jnp.float32),
            dma((windows,)), dma((windows,)), dma((windows,)), dma((windows,)),
        ],
        compiler_params=pltpu.CompilerParams(collective_id=1, has_side_effects=True),
    )(lagged, sent, decay)
    return stacked.reshape(1, stations, slots * stations, LAGS)


def solution(mesh):
    in_specs = (
        P("section", "sta", None, None),
        P("section", "sta", None),
        P("sta", None),
        P("section"),
    )
    out_specs = P("section", "sta", None, None)
    sizes = (mesh.shape["sta"], mesh.shape["section"])
    return jax.shard_map(
        functools.partial(body, sizes), mesh=mesh, in_specs=in_specs, out_specs=out_specs, check_vma=False
    )
```

profile of v0, /device:TPU:0, one launch (start us, length us, event | category | flops | bytes accessed | tf_op | source)
XLA Modules:
  0.0 58.1 jit_solution(14946201033700520278)
XLA Ops:
  0.0 0.7 %fusion = (bf16[8,8]{1,0:T(8,128)(2,1)S(1)}, f32[8,8]{1,0:T(8,128)S(1)}) fusion(s32[1,8,8]{2,1,0:T(8,128)} %param.9), kind=kLoop, calls=%fused_computation.1 | loop fusion | flops 128 | bytes 640 | tf_op jit(solution)/shard_map/convert
  0.7 0.7 %broadcast_in_dim.6.mask_ref = f32[8,8,128]{2,1,0:T(8,128)} broadcast(f32[8,8]{1,0:T(8,128)S(1)} %get-tuple-element.10), dimensions={0,1} | broadcast | bytes 33024 | tf_op jit(solution)/shard_map/broadcast_in_dim | solution.py:289
  1.4 0.6 %pad.5.row_ref = bf16[16,128]{1,0:T(8,128)(2,1)} pad(bf16[8,8]{1,0:T(8,128)(2,1)S(1)} %get-tuple-element.9, bf16[]{:T(256)} %constant.11.clone.1), padding=0_8x0_120 | pad | bytes 4226 | tf_op jit(solution)/shard_map/jit(_pad)/pad | solution.py:290
  2.0 4.8 %spectrum.1.own_ref = bf16[65,16,128]{2,1,0:T(8,128)(2,1)} custom-call(bf16[1,8,8,4096]{3,2,1,0:T(8,128)(2,1)} %x_ref.1, f32[8,8,128]{2,1,0:T(8,128)} %broadcast_in_dim.6.mask_ref, bf16[16,128]{1,0:T(8,128)(2,1)} %pad.5.row_ref, bf16[1024,256]{1,0:T(8,128)(2,1)} %constant.12.clone.high_ref, bf16[1024,256]{1,0:T(8,128)(2,1)} %constant.13.clone.low_ref, ...), custom_call_target="tpu_custom_call" | custom-call | tf_op jit(solution)/shard_map/spectrum/pallas_call | solution.py:295
  6.7 28.6 %gather.1.all_ref = bf16[8,65,16,128]{3,2,1,0:T(8,128)(2,1)} custom-call(bf16[65,16,128]{2,1,0:T(8,128)(2,1)} %spectrum.1.own_ref), custom_call_target="tpu_custom_call" | custom-call | tf_op jit(solution)/shard_map/gather/pallas_call | solution.py:308
  35.3 6.4 %cross.1 = (f32[256,384]{1,0:T(8,128)}, bf16[256,384]{1,0:T(8,128)(2,1)}) custom-call(s32[1,4]{1,0:T(1,128)} %pair_ref.1, bf16[65,16,128]{2,1,0:T(8,128)(2,1)} %spectrum.1.own_ref, bf16[8,65,16,128]{3,2,1,0:T(8,128)(2,1)} %gather.1.all_ref, bf16[8,256,384]{2,1,0:T(8,128)(2,1)} %constant.15.clone.table_ref), custom_call_target="tpu_custom_call" | custom-call | tf_op jit(solution)/shard_map/cross/pallas_call | solution.py:318
  42.4 0.6 %broadcast_in_dim.16.decay_ref = f32[8,128]{1,0:T(8,128)} broadcast(f32[]{:T(128)} %bitcast.6), dimensions={} | broadcast | bytes 4100 | tf_op jit(solution)/shard_map/broadcast_in_dim | solution.py:333
  43.0 13.5 %stack.1 = bf16[256,384]{1,0:T(8,128)(2,1)} custom-call(f32[256,384]{1,0:T(8,128)} %get-tuple-element.7.lag_ref, bf16[256,384]{1,0:T(8,128)(2,1)} %get-tuple-element.8.send_ref, f32[8,128]{1,0:T(8,128)} %broadcast_in_dim.16.decay_ref), custom_call_target="tpu_custom_call" | custom-call | tf_op jit(solution)/shard_map/stack/pallas_call | solution.py:334
  56.5 1.6 %copy.11 = bf16[1,8,32,384]{3,2,1,0:T(8,128)(2,1)} copy(bf16[1,8,32,384]{3,2,1,0:T(8,128)(2,1)} %bitcast.7) | data formatting | bytes 393216
where the time goes:
time: 58.4 us; the launch traced here: 58.1 us
  Pallas kernels  53.3 us (91%)
  local copies, waits for them, and re-layouts  3.5 us (6%)
  other arithmetic  0.69 us (1%)
  between operations  0.67 us (1%)
    pallas_call x1, Pallas kernels, body(): pl.pallas_call(functools.partial(gather_kernel, n), name='gather', out_sh...  28.6 us
    pallas_call x1, Pallas kernels, body(): pl.pallas_call(functools.partial(stack_kernel, windows), name='stack', ou...  13.5 us
    pallas_call x1, Pallas kernels, body(): pl.pallas_call(functools.partial(cross_kernel, stations, slots), name='cr...  6.43 us
    pallas_call x1, Pallas kernels, body(): pl.pallas_call(functools.partial(spectrum_kernel, stations), name='spectr...  4.77 us
    unnamed x1, local copies, waits for them, and re-layouts  1.62 us

commit v1 on v0

v1 whole, which is shorter than its diff:
```python
import functools
import math

import jax
import jax.numpy as jnp
import numpy as np
from jax import lax
from jax.experimental import pallas as pl
from jax.experimental.pallas import tpu as pltpu
from jax.sharding import PartitionSpec as P

MESH = pl.DeviceIdType.MESH
RADIX = 64
NF = 1024
LAGS = 384
SMOOTH_HALF = 32
LANES = 128
SUB = 8
EPSILON = 1e-05
NSAMP = RADIX * RADIX
FIRST = NSAMP // LANES
SLICES = FIRST // SUB
BINS = NF // FIRST


def dft_tables():
    b = np.arange(LANES)
    m = np.arange(BINS)
    phi = 2.0 * np.pi * ((b[:, None] * (m[None, :] + 2 * RADIX // FIRST)) % LANES) / LANES
    table = np.zeros((SLICES, 2, LANES, 2, BINS, SLICES))
    for q in range(SLICES):
        table[q, 0, :, 0, :, q] = np.cos(phi)
        table[q, 1, :, 0, :, q] = np.sin(phi)
        table[q, 0, :, 1, :, q] = -np.sin(phi)
        table[q, 1, :, 1, :, q] = np.cos(phi)
    table = (table / RADIX).reshape(SLICES * 2 * LANES, 2 * BINS * SLICES).astype(np.float32)
    high = table.astype(jnp.bfloat16)
    low = (table - high.astype(np.float32)).astype(jnp.bfloat16)
    turn = 2.0 * np.pi * np.arange(FIRST)[:, None] * b[None, :] / NSAMP
    twist = np.stack([np.cos(turn), np.sin(turn)], axis=1).astype(np.float32)
    return high, low, twist


def lag_table():
    f = SUB * np.arange(NF // SUB)[None, :] + np.arange(SUB)[:, None]
    shift = np.arange(LAGS) + NSAMP - LAGS // 2
    theta = 2.0 * np.pi * (((2 * RADIX + f)[:, :, None] * shift) % NSAMP) / NSAMP
    table = np.concatenate([np.cos(theta), -np.sin(theta)], axis=1) / math.sqrt(NF)
    return table.astype(np.float32).astype(jnp.bfloat16)


def real_dft(values):
    size = len(values)
    if size == 1:
        return [(values[0], None)]
    if size == 2:
        return [(values[0] + values[1], None), (values[0] - values[1], None)]
    even, odd = real_dft(values[0::2]), real_dft(values[1::2])
    half = size // 2
    out = [None] * (half + 1)
    for k in range(half // 2 + 1):
        er, ei = even[k]
        pr, pi = odd[k]
        if k == 0:
            out[0] = (er + pr, None)
            out[half] = (er - pr, None)
            continue
        if k * 4 == size:
            out[k] = (er, -pr)
            continue
        c, s = math.cos(2 * math.pi * k / size), math.sin(2 * math.pi * k / size)
        tr, ti = pr * c + pi * s, pi * c - pr * s
        out[k] = (er + tr, ei + ti)
        out[half - k] = (er - tr, ti - ei)
    return out


def spectrum_kernel(stations, x_ref, mask_ref, high_ref, low_ref, twist_ref, out_ref, y_ref, z_ref, w_ref, row_ref):
    rows = stations * SUB

    def first(st, _):
        pieces = [x_ref[0, st, :, a * LANES:(a + 1) * LANES].astype(jnp.float32) for a in range(FIRST)]
        spread = real_dft(pieces)
        base = pl.multiple_of(st * SUB, SUB)
        for k1 in range(FIRST):
            re, im = spread[k1] if 2 * k1 <= FIRST else spread[FIRST - k1]
            c, s = twist_ref[k1, 0:1, :], twist_ref[k1, 1:2, :]
            if im is None:
                yr, yi = re * c, -(re * s)
            elif 2 * k1 <= FIRST:
                yr, yi = re * c + im * s, im * c - re * s
            else:
                yr, yi = re * c - im * s, -(im * c) - re * s
            q, p = k1 // SUB, k1 % SUB
            y_ref[pl.ds(p * rows + base, SUB), 2 * q * LANES:(2 * q + 1) * LANES] = yr
            y_ref[pl.ds(p * rows + base, SUB), (2 * q + 1) * LANES:(2 * q + 2) * LANES] = yi
        return 0

    lax.fori_loop(0, stations, first, 0)
    y = y_ref[...]
    yh = y.astype(jnp.bfloat16)
    yl = (y - yh.astype(jnp.float32)).astype(jnp.bfloat16)
    dot = functools.partial(jnp.dot, preferred_element_type=jnp.float32)
    z_ref[...] = dot(yh, high_ref[...]) + dot(yl, high_ref[...]) + dot(yh, low_ref[...])
    reach = SMOOTH_HALF // SUB
    square = lax.broadcasted_iota(jnp.int32, (SUB, SUB), 0) == lax.broadcasted_iota(jnp.int32, (SUB, SUB), 1)

    def second(st, _):
        base = pl.multiple_of(st * SUB, SUB)
        lane = lax.broadcasted_iota(jnp.int32, (SUB, LANES), 1)

        def moved(v, d):
            inside = (lane + d >= 0) & (lane + d < LANES)
            return jnp.where(inside, pltpu.roll(v, (-d) % LANES, 1), 0.0)

        re = [z_ref[pl.ds(p * rows + base, SUB), 0:LANES] for p in range(SUB)]
        im = [z_ref[pl.ds(p * rows + base, SUB), LANES:2 * LANES] for p in range(SUB)]
        amp = [jnp.sqrt(re[p] * re[p] + im[p] * im[p]) for p in range(SUB)]
        pre = [amp[0]]
        for p in range(1, SUB):
            pre.append(pre[-1] + amp[p])
        suf = [amp[SUB - 1]]
        for p in range(SUB - 2, -1, -1):
            suf.insert(0, suf[0] + amp[p])
        middle = pre[-1]
        for d in range(1, reach):
            middle = middle + moved(pre[-1], d) + moved(pre[-1], -d)
        row = jnp.broadcast_to(mask_ref[0, pl.ds(st, 1), :].astype(jnp.float32), (SUB, SUB))
        marks = jnp.sum(jnp.where(square, row, 0.0), axis=1, keepdims=True)
        for p in range(SUB):
            smooth = (middle + moved(suf[p], -reach) + moved(pre[p], reach)) / (2 * SMOOTH_HALF + 1)
            scale = marks / (smooth + EPSILON)
            w_ref[pl.ds(p, SUB, stride=2 * SUB), :] = re[p] * scale
            w_ref[pl.ds(SUB + p, SUB, stride=2 * SUB), :] = im[p] * scale
        out_ref[pl.ds(1 + base, SUB)] = w_ref[...].reshape(SUB, 2 * SUB, LANES).astype(jnp.bfloat16)
        return 0

    lax.fori_loop(0, stations, second, 0)
    row_ref[...] = jnp.zeros_like(row_ref)
    row_ref[0:stations, 0:SUB] = mask_ref[0].astype(jnp.float32)
    out_ref[0] = row_ref[...].astype(jnp.bfloat16)


CHUNKS = 4


def correlate_kernel(n, windows, stations, slots, pair_ref, decay_ref, own_ref, table_ref, out_ref, *scratch):
    bufs = scratch[:CHUNKS]
    (loc_ref, cr_ref, ci_ref, inv_ref, lag_ref, send_ref, got_ref, mine_ref, rate_ref, full_ref, rail_send, rail_recv,
     mate_send, mate_recv, lag_send, lag_recv, rate_send, rate_recv) = scratch[CHUNKS:]
    me, window = lax.axis_index("sta"), lax.axis_index("section")
    length = n // 2
    core, place = lax.rem(me, 2), me // 2
    mate = place * 2 + 1 - core
    segments = SUB
    wide = stations // CHUNKS
    pairs = stations * slots
    mine_ref[...] = jnp.full(mine_ref.shape, decay_ref[0], jnp.float32)

    barrier = pltpu.get_barrier_semaphore()
    has_right, has_left = place < length - 1, place > 0

    def greet(peer):
        pl.semaphore_signal(barrier, inc=1, device_id=peer, device_id_type=MESH)

    greet({"sta": mate})
    for d in range(1, windows):
        greet({"section": lax.rem(window + d, windows)})

    @pl.when(has_right)
    def _():
        greet({"sta": me + 2})

    @pl.when(has_left)
    def _():
        greet({"sta": me - 2})

    pl.semaphore_wait(barrier, windows + jnp.where(has_right, 1, 0) + jnp.where(has_left, 1, 0))

    def span(c):
        return pl.ds(0 if c == 0 else 1 + c * wide * segments, wide * segments + (1 if c == 0 else 0))

    def rail(c, d, way):
        origin = me - 2 * way * d
        src = own_ref.at[span(c)] if d == 0 else bufs[c].at[origin]
        at = (c * length + d) * 2 + (1 + way) // 2
        return pltpu.make_async_remote_copy(
            src_ref=src, dst_ref=bufs[c].at[origin], send_sem=rail_send.at[at], recv_sem=rail_recv.at[at],
            device_id={"sta": me + 2 * way}, device_id_type=MESH)

    def landed(c, d, way):
        origin = me - 2 * way * d
        at = (c * length + d - 1) * 2 + (1 + way) // 2
        return pltpu.make_async_remote_copy(
            src_ref=bufs[c].at[origin], dst_ref=bufs[c].at[origin], send_sem=rail_send.at[at],
            recv_sem=rail_recv.at[at], device_id={"sta": me + 2 * way}, device_id_type=MESH)

    def across(c, origin_place, sender_core):
        origin = origin_place * 2 + sender_core
        at = c * length + origin_place
        return pltpu.make_async_remote_copy(
            src_ref=bufs[c].at[origin], dst_ref=bufs[c].at[origin], send_sem=mate_send.at[at],
            recv_sem=mate_recv.at[at], device_id={"sta": mate}, device_id_type=MESH)

    def own_across(c):
        at = c * length + place
        return pltpu.make_async_remote_copy(
            src_ref=own_ref.at[span(c)], dst_ref=bufs[c].at[me], send_sem=mate_send.at[at],
            recv_sem=mate_recv.at[at], device_id={"sta": mate}, device_id_type=MESH)

    def onward(way, d):
        return (place - way * d >= 0) & (place - way * d < length) & (place + way >= 0) & (place + way < length)

    def holds(way, d):
        return (place - way * d >= 0) & (place - way * d < length)

    def send_own(c):
        for way in (1, -1):
            @pl.when(onward(way, 0))
            def _():
                rail(c, 0, way).start()
        own_across(c).start()

    def later(c, d):
        return (
            pltpu.make_async_remote_copy(
                src_ref=send_ref.at[c], dst_ref=got_ref.at[window, c], send_sem=lag_send.at[d * CHUNKS + c],
                recv_sem=lag_recv.at[window * CHUNKS + c], device_id={"section": window + d}, device_id_type=MESH))

    def earlier(c, v):
        return pltpu.make_async_remote_copy(
            src_ref=send_ref.at[c], dst_ref=got_ref.at[v, c], send_sem=lag_send.at[c],
            recv_sem=lag_recv.at[v * CHUNKS + c], device_id={"section": v}, device_id_type=MESH)

    def rate_later(d):
        return pltpu.make_async_remote_copy(
            src_ref=mine_ref, dst_ref=rate_ref.at[window], send_sem=rate_send.at[d],
            recv_sem=rate_recv.at[window], device_id={"section": window + d}, device_id_type=MESH)

    def rate_earlier(v):
        return pltpu.make_async_remote_copy(
            src_ref=mine_ref, dst_ref=rate_ref.at[v], send_sem=rate_send.at[0],
            recv_sem=rate_recv.at[v], device_id={"section": v}, device_id_type=MESH)

    ahead = 2
    for c in range(min(ahead, CHUNKS)):
        send_own(c)
    for d in range(1, windows):
        @pl.when(window + d < windows)
        def _():
            rate_later(d).start()
    for c in range(CHUNKS):
        bufs[c][me] = own_ref[span(c)]
    loc_ref[...] = own_ref[1:1 + stations * segments].astype(jnp.float32)

    def combine(c):
        rows = wide * pairs
        full_ref[...] = jnp.zeros_like(full_ref)
        for v in range(windows - 1):
            @pl.when(v < window)
            def _():
                if c == 0:
                    rate_earlier(v).wait_recv()
                earlier(c, v).wait_recv()
                full_ref[...] = full_ref[...] * rate_ref[v, 0:1, 0:1] + got_ref[v, c].astype(jnp.float32)
        total = full_ref[...] * mine_ref[0:1, 0:1] + lag_ref[c * rows:(c + 1) * rows, :]
        for jj in range(wide):
            for part in range(LAGS // LANES):
                cols = slice(part * LANES, (part + 1) * LANES)
                inv_ref[1 + part, pl.ds(c * wide + jj, pairs, stride=stations), :] = total[jj * pairs:(jj + 1) * pairs, cols]

    for c in range(CHUNKS):
        for d in range(1, length):
            for way in (1, -1):
                @pl.when(holds(way, d))
                def _():
                    landed(c, d, way).wait_recv()
                    across(c, place - way * d, core).start()

                @pl.when(onward(way, d))
                def _():
                    rail(c, d, way).start()
            if d == 1 and c + ahead < CHUNKS:
                send_own(c + ahead)
        for origin in range(length):
            across(c, origin, 1 - core).wait_recv()
        first = 1 if c == 0 else 0
        if c == 0:
            mine = own_ref[0].astype(jnp.float32)
            for k in range(slots):
                theirs = bufs[0][pair_ref[0, k], 0].astype(jnp.float32)[0:stations]
                for i in range(stations):
                    count = jnp.sum(mine[i:i + 1] * theirs, axis=1, keepdims=True)
                    at = (i * slots + k) * stations
                    inv_ref[0, at:at + stations, :] = jnp.broadcast_to(1.0 / jnp.maximum(count, 1.0), (stations, LANES))

        def pair(t, _):
            k, jj = t // wide, lax.rem(t, wide)
            block = pair_ref[0, k]
            other = [bufs[c][block, first + jj * segments + s].astype(jnp.float32) for s in range(segments)]
            for i in range(stations):
                re = im = None
                for s in range(segments):
                    ar, ai = loc_ref[i * segments + s, 0:SUB, :], loc_ref[i * segments + s, SUB:2 * SUB, :]
                    br, bi = other[s][0:SUB], other[s][SUB:2 * SUB]
                    tr, ti = ar * br + ai * bi, ar * bi - ai * br
                    re, im = (tr, ti) if re is None else (re + tr, im + ti)
                at = pl.ds(pl.multiple_of((jj * pairs + i * slots + k) * SUB, SUB), SUB)
                cr_ref[at, :] = re
                ci_ref[at, :] = im
            return 0

        lax.fori_loop(0, slots * wide, pair, 0)
        rows = wide * pairs
        acc = None
        for p in range(SUB):
            at = pl.ds(p, rows, stride=SUB)
            lhs = jnp.concatenate([cr_ref[at, :], ci_ref[at, :]], axis=1).astype(jnp.bfloat16)
            term = jnp.dot(lhs, table_ref[p], preferred_element_type=jnp.float32)
            acc = term if acc is None else acc + term
        for jj in range(wide):
            inv = inv_ref[0, pl.ds(c * wide + jj, pairs, stride=stations), :]
            value = acc[jj * pairs:(jj + 1) * pairs] * jnp.concatenate([inv] * (LAGS // LANES), axis=1)
            lag_ref[c * rows + jj * pairs:c * rows + (jj + 1) * pairs, :] = value
            send_ref[c, jj * pairs:(jj + 1) * pairs, :] = value.astype(jnp.bfloat16)
        for d in range(1, windows):
            @pl.when(window + d < windows)
            def _():
                later(c, d).start()
        if c > 0:
            combine(c - 1)
    combine(CHUNKS - 1)
    for part in range(LAGS // LANES):
        out_ref[:, part * LANES:(part + 1) * LANES] = inv_ref[1 + part].astype(jnp.bfloat16)
    for c in range(CHUNKS):
        for d in range(length):
            for way in (1, -1):
                @pl.when(onward(way, d))
                def _():
                    rail(c, d, way).wait_send()
        for origin in range(length):
            across(c, origin, core).wait_send()
        for d in range(1, windows):
            @pl.when(window + d < windows)
            def _():
                later(c, d).wait_send()
    for d in range(1, windows):
        @pl.when(window + d < windows)
        def _():
            rate_later(d).wait_send()


def body(sizes, waveforms, segment_mask, pair_blocks, window_decay):
    n, windows = sizes
    stations, segments = waveforms.shape[1], waveforms.shape[2]
    slots = pair_blocks.shape[1]
    rows = stations * segments
    high, low, twist = dft_tables()
    vmem = pl.BlockSpec(memory_space=pltpu.VMEM)
    smem = pl.BlockSpec(memory_space=pltpu.SMEM)
    own = pl.pallas_call(
        functools.partial(spectrum_kernel, stations),
        name="spectrum",
        out_shape=jax.ShapeDtypeStruct((1 + rows, 2 * SUB, LANES), jnp.bfloat16),
        in_specs=[vmem] * 5,
        out_specs=vmem,
        scratch_shapes=[
            pltpu.VMEM((SUB * rows, SLICES * 2 * LANES), jnp.float32),
            pltpu.VMEM((SUB * rows, 2 * LANES), jnp.float32),
            pltpu.VMEM((SUB * 2 * SUB, LANES), jnp.float32),
            pltpu.VMEM((2 * SUB, LANES), jnp.float32),
        ],
    )(waveforms, segment_mask, jnp.asarray(high), jnp.asarray(low), jnp.asarray(twist))
    dma = pltpu.SemaphoreType.DMA
    total = stations * slots * stations
    part = total // CHUNKS
    length = n // 2
    bufs = [
        pltpu.VMEM((n, rows // CHUNKS + (1 if c == 0 else 0), 2 * SUB, LANES), jnp.bfloat16) for c in range(CHUNKS)
    ]
    stacked = pl.pallas_call(
        functools.partial(correlate_kernel, n, windows, stations, slots),
        name="correlate",
        out_shape=jax.ShapeDtypeStruct((total, LAGS), jnp.bfloat16),
        in_specs=[smem, smem, vmem, vmem],
        out_specs=vmem,
        scratch_shapes=bufs + [
            pltpu.VMEM((rows, 2 * SUB, LANES), jnp.float32),
            pltpu.VMEM((part * SUB, LANES), jnp.float32),
            pltpu.VMEM((part * SUB, LANES), jnp.float32),
            pltpu.VMEM((1 + LAGS // LANES, total, LANES), jnp.float32),
            pltpu.VMEM((total, LAGS), jnp.float32),
            pltpu.VMEM((CHUNKS, part, LAGS), jnp.bfloat16),
            pltpu.VMEM((windows, CHUNKS, part, LAGS), jnp.bfloat16),
            pltpu.VMEM((SUB, LANES), jnp.float32),
            pltpu.VMEM((windows, SUB, LANES), jnp.float32),
            pltpu.VMEM((part, LAGS), jnp.float32),
            dma((2 * CHUNKS * length,)), dma((2 * CHUNKS * length,)),
            dma((CHUNKS * length,)), dma((CHUNKS * length,)),
            dma((windows * CHUNKS,)), dma((windows * CHUNKS,)),
            dma((windows,)), dma((windows,)),
        ],
        compiler_params=pltpu.CompilerParams(collective_id=0, has_side_effects=True),
    )(pair_blocks, window_decay, own, jnp.asarray(lag_table()))
    return stacked.reshape(1, stations, slots * stations, LAGS)


def solution(mesh):
    in_specs = (
        P("section", "sta", None, None),
        P("section", "sta", None),
        P("sta", None),
        P("section"),
    )
    out_specs = P("section", "sta", None, None)
    sizes = (mesh.shape["sta"], mesh.shape["section"])
    return jax.shard_map(
        functools.partial(body, sizes), mesh=mesh, in_specs=in_specs, out_specs=out_specs, check_vma=False
    )
```

time: 58.4 us -> 46.3 us (0.79)
  Pallas kernels: 53.3 us -> 43.8 us
  local copies, waits for them, and re-layouts: 3.5 us -> 1.62 us
  other arithmetic: 0.69 us -> 0 us
    pallas_call x3 -> x1, Pallas kernels: 48.5 us -> 39 us  [body(): pl.pallas_call(functools.partial(correlate_kernel, n, windows, stations,...]
    broadcast_in_dim x2 -> x0, local copies, waits for them, and re-layouts: 1.28 us -> none  [the longest x1 0.69 us: body(): jnp.broadcast_to(marks[:, :, None], (stations, segments, LANES))]
    another operation x1 -> x0, other arithmetic: 0.69 us -> none
    pad x1 -> x0, local copies, waits for them, and re-layouts: 0.59 us -> none  [body(): jnp.pad(marks, ((0, 2 * SUB - stations), (0, LANES - segments)))]
where the time goes in v1:
time: 46.3 us; the launch traced here: 46.1 us
  Pallas kernels  43.8 us (95%)
  local copies, waits for them, and re-layouts  1.62 us (3%)
  between operations  0.66 us (1%)
    pallas_call x1, Pallas kernels, body(): pl.pallas_call(functools.partial(correlate_kernel, n, windows, stations,...  39 us
    pallas_call x1, Pallas kernels, body(): pl.pallas_call(functools.partial(spectrum_kernel, stations), name='spectr...  4.87 us
    unnamed x1, local copies, waits for them, and re-layouts  1.62 us

profile of v1, /device:TPU:0, one launch (start us, length us, event | category | flops | bytes accessed | tf_op | source)
XLA Modules:
  0.0 46.1 jit_solution(6247161422976328987)
XLA Ops:
  0.7 4.9 %spectrum.1.own_ref = bf16[65,16,128]{2,1,0:T(8,128)(2,1)} custom-call(bf16[1,8,8,4096]{3,2,1,0:T(8,128)(2,1)} %x_ref.1, s32[1,8,8]{2,1,0:T(8,128)} %mask_ref.1, bf16[1024,256]{1,0:T(8,128)(2,1)} %constant.8.clone.high_ref, bf16[1024,256]{1,0:T(8,128)(2,1)} %constant.9.clone.low_ref, f32[32,2,128]{2,1,0:T(2,128)} %constant.10.clone.twist_ref), custom_call_target="tpu_custom_call" | custom-call | tf_op jit(solution)/shard_map/spectrum/pallas_call | solution.py:361
  5.5 39.0 %correlate.1 = bf16[256,384]{1,0:T(8,128)(2,1)} custom-call(s32[1,4]{1,0:T(1,128)} %pair_ref.1, f32[1]{0:T(128)S(6)} %copy.10.decay_ref, bf16[65,16,128]{2,1,0:T(8,128)(2,1)} %spectrum.1.own_ref, bf16[8,256,384]{2,1,0:T(8,128)(2,1)} %constant.11.clone.table_ref), custom_call_target="tpu_custom_call" | custom-call | tf_op jit(solution)/shard_map/correlate/pallas_call | solution.py:381
  44.5 1.6 %copy.11 = bf16[1,8,32,384]{3,2,1,0:T(8,128)(2,1)} copy(bf16[1,8,32,384]{3,2,1,0:T(8,128)(2,1)} %bitcast.1) | data formatting | bytes 393216

commit v2 on v1

--- a/solution.py
+++ b/solution.py
@@ -269,19 +269,27 @@
                 cols = slice(part * LANES, (part + 1) * LANES)
                 inv_ref[1 + part, pl.ds(c * wide + jj, pairs, stride=stations), :] = total[jj * pairs:(jj + 1) * pairs, cols]
 
-    for c in range(CHUNKS):
+    def relay(c):
         for d in range(1, length):
             for way in (1, -1):
                 @pl.when(holds(way, d))
                 def _():
                     landed(c, d, way).wait_recv()
-                    across(c, place - way * d, core).start()
 
                 @pl.when(onward(way, d))
                 def _():
                     rail(c, d, way).start()
+
+                @pl.when(holds(way, d))
+                def _():
+                    across(c, place - way * d, core).start()
             if d == 1 and c + ahead < CHUNKS:
                 send_own(c + ahead)
+
+    relay(0)
+    for c in range(CHUNKS):
+        if c + 1 < CHUNKS:
+            relay(c + 1)
         for origin in range(length):
             across(c, origin, 1 - core).wait_recv()
         first = 1 if c == 0 else 0

time: 46.3 us -> 43.5 us (0.940)
  Pallas kernels: 43.8 us -> 40.8 us
    pallas_call x1, Pallas kernels: 39 us -> 35.9 us  [body(): pl.pallas_call(functools.partial(correlate_kernel, n, windows, stations,...]
where the time goes in v2:
time: 43.5 us; the launch traced here: 43.1 us
  Pallas kernels  40.8 us (94%)
  local copies, waits for them, and re-layouts  1.62 us (4%)
  between operations  0.66 us (2%)
    pallas_call x1, Pallas kernels, body(): pl.pallas_call(functools.partial(correlate_kernel, n, windows, stations,...  35.9 us
    pallas_call x1, Pallas kernels, body(): pl.pallas_call(functools.partial(spectrum_kernel, stations), name='spectr...  4.87 us
    unnamed x1, local copies, waits for them, and re-layouts  1.62 us

profile of v2, /device:TPU:0, one launch (start us, length us, event | category | flops | bytes accessed | tf_op | source)
XLA Modules:
  0.0 43.1 jit_solution(5641846433940768458)
XLA Ops:
  0.7 4.9 %spectrum.1.own_ref = bf16[65,16,128]{2,1,0:T(8,128)(2,1)} custom-call(bf16[1,8,8,4096]{3,2,1,0:T(8,128)(2,1)} %x_ref.1, s32[1,8,8]{2,1,0:T(8,128)} %mask_ref.1, bf16[1024,256]{1,0:T(8,128)(2,1)} %constant.8.clone.high_ref, bf16[1024,256]{1,0:T(8,128)(2,1)} %constant.9.clone.low_ref, f32[32,2,128]{2,1,0:T(2,128)} %constant.10.clone.twist_ref), custom_call_target="tpu_custom_call" | custom-call | tf_op jit(solution)/shard_map/spectrum/pallas_call | solution.py:369
  5.5 35.9 %correlate.1 = bf16[256,384]{1,0:T(8,128)(2,1)} custom-call(s32[1,4]{1,0:T(1,128)} %pair_ref.1, f32[1]{0:T(128)S(6)} %copy.10.decay_ref, bf16[65,16,128]{2,1,0:T(8,128)(2,1)} %spectrum.1.own_ref, bf16[8,256,384]{2,1,0:T(8,128)(2,1)} %constant.11.clone.table_ref), custom_call_target="tpu_custom_call" | custom-call | tf_op jit(solution)/shard_map/correlate/pallas_call | solution.py:389
  41.4 1.6 %copy.11 = bf16[1,8,32,384]{3,2,1,0:T(8,128)(2,1)} copy(bf16[1,8,32,384]{3,2,1,0:T(8,128)(2,1)} %bitcast.1) | data formatting | bytes 393216

commit v3 on v2

--- a/solution.py
+++ b/solution.py
@@ -75,11 +75,11 @@
     return out
 
 
-def spectrum_kernel(stations, x_ref, mask_ref, high_ref, low_ref, twist_ref, out_ref, y_ref, z_ref, w_ref, row_ref):
-    rows = stations * SUB
+def spectrum(begin, count, x_ref, mask_ref, high_ref, low_ref, twist_ref, out_ref, y_ref, z_ref, w_ref):
+    rows = count * SUB
 
     def first(st, _):
-        pieces = [x_ref[0, st, :, a * LANES:(a + 1) * LANES].astype(jnp.float32) for a in range(FIRST)]
+        pieces = [x_ref[0, begin + st, :, a * LANES:(a + 1) * LANES].astype(jnp.float32) for a in range(FIRST)]
         spread = real_dft(pieces)
         base = pl.multiple_of(st * SUB, SUB)
         for k1 in range(FIRST):
@@ -96,7 +96,7 @@
             y_ref[pl.ds(p * rows + base, SUB), (2 * q + 1) * LANES:(2 * q + 2) * LANES] = yi
         return 0
 
-    lax.fori_loop(0, stations, first, 0)
+    lax.fori_loop(0, count, first, 0)
     y = y_ref[...]
     yh = y.astype(jnp.bfloat16)
     yl = (y - yh.astype(jnp.float32)).astype(jnp.bfloat16)
@@ -125,29 +125,27 @@
         middle = pre[-1]
         for d in range(1, reach):
             middle = middle + moved(pre[-1], d) + moved(pre[-1], -d)
-        row = jnp.broadcast_to(mask_ref[0, pl.ds(st, 1), :].astype(jnp.float32), (SUB, SUB))
+        row = jnp.broadcast_to(mask_ref[0, pl.ds(begin + st, 1), :].astype(jnp.float32), (SUB, SUB))
         marks = jnp.sum(jnp.where(square, row, 0.0), axis=1, keepdims=True)
         for p in range(SUB):
             smooth = (middle + moved(suf[p], -reach) + moved(pre[p], reach)) / (2 * SMOOTH_HALF + 1)
             scale = marks / (smooth + EPSILON)
             w_ref[pl.ds(p, SUB, stride=2 * SUB), :] = re[p] * scale
             w_ref[pl.ds(SUB + p, SUB, stride=2 * SUB), :] = im[p] * scale
-        out_ref[pl.ds(1 + base, SUB)] = w_ref[...].reshape(SUB, 2 * SUB, LANES).astype(jnp.bfloat16)
+        out_ref[pl.ds(1 + begin * SUB + base, SUB)] = w_ref[...].reshape(SUB, 2 * SUB, LANES).astype(jnp.bfloat16)
         return 0
 
-    lax.fori_loop(0, stations, second, 0)
-    row_ref[...] = jnp.zeros_like(row_ref)
-    row_ref[0:stations, 0:SUB] = mask_ref[0].astype(jnp.float32)
-    out_ref[0] = row_ref[...].astype(jnp.bfloat16)
+    lax.fori_loop(0, count, second, 0)
 
 
 CHUNKS = 4
 
 
-def correlate_kernel(n, windows, stations, slots, pair_ref, decay_ref, own_ref, table_ref, out_ref, *scratch):
+def correlate_kernel(n, windows, stations, slots, pair_ref, decay_ref, x_ref, mask_ref, high_ref,
+                     low_ref, twist_ref, table_ref, out_ref, *scratch):
     bufs = scratch[:CHUNKS]
     (loc_ref, cr_ref, ci_ref, inv_ref, lag_ref, send_ref, got_ref, mine_ref, rate_ref, full_ref, rail_send, rail_recv,
-     mate_send, mate_recv, lag_send, lag_recv, rate_send, rate_recv) = scratch[CHUNKS:]
+     mate_send, mate_recv, lag_send, lag_recv, rate_send, rate_recv, own_ref, y_ref, z_ref, w_ref, row_ref) = scratch[CHUNKS:]
     me, window = lax.axis_index("sta"), lax.axis_index("section")
     length = n // 2
     core, place = lax.rem(me, 2), me // 2
@@ -175,6 +173,13 @@
     def _():
         greet({"sta": me - 2})
 
+    def transform(c):
+        spectrum(c * wide, wide, x_ref, mask_ref, high_ref, low_ref, twist_ref, own_ref, y_ref, z_ref, w_ref)
+
+    row_ref[...] = jnp.zeros_like(row_ref)
+    row_ref[0:stations, 0:SUB] = mask_ref[0].astype(jnp.float32)
+    own_ref[0] = row_ref[...].astype(jnp.bfloat16)
+    transform(0)
     pl.semaphore_wait(barrier, windows + jnp.where(has_right, 1, 0) + jnp.where(has_left, 1, 0))
 
     def span(c):
@@ -243,12 +248,15 @@
             recv_sem=rate_recv.at[v], device_id={"section": v}, device_id_type=MESH)
 
     ahead = 2
-    for c in range(min(ahead, CHUNKS)):
-        send_own(c)
+    send_own(0)
     for d in range(1, windows):
         @pl.when(window + d < windows)
         def _():
             rate_later(d).start()
+    for c in range(1, CHUNKS):
+        transform(c)
+        if 1 <= c - 1 < ahead:
+            send_own(c - 1)
     for c in range(CHUNKS):
         bufs[c][me] = own_ref[span(c)]
     loc_ref[...] = own_ref[1:1 + stations * segments].astype(jnp.float32)
@@ -366,19 +374,6 @@
     high, low, twist = dft_tables()
     vmem = pl.BlockSpec(memory_space=pltpu.VMEM)
     smem = pl.BlockSpec(memory_space=pltpu.SMEM)
-    own = pl.pallas_call(
-        functools.partial(spectrum_kernel, stations),
-        name="spectrum",
-        out_shape=jax.ShapeDtypeStruct((1 + rows, 2 * SUB, LANES), jnp.bfloat16),
-        in_specs=[vmem] * 5,
-        out_specs=vmem,
-        scratch_shapes=[
-            pltpu.VMEM((SUB * rows, SLICES * 2 * LANES), jnp.float32),
-            pltpu.VMEM((SUB * rows, 2 * LANES), jnp.float32),
-            pltpu.VMEM((SUB * 2 * SUB, LANES), jnp.float32),
-            pltpu.VMEM((2 * SUB, LANES), jnp.float32),
-        ],
-    )(waveforms, segment_mask, jnp.asarray(high), jnp.asarray(low), jnp.asarray(twist))
     dma = pltpu.SemaphoreType.DMA
     total = stations * slots * stations
     part = total // CHUNKS
@@ -390,7 +385,7 @@
         functools.partial(correlate_kernel, n, windows, stations, slots),
         name="correlate",
         out_shape=jax.ShapeDtypeStruct((total, LAGS), jnp.bfloat16),
-        in_specs=[smem, smem, vmem, vmem],
+        in_specs=[smem, smem] + [vmem] * 6,
         out_specs=vmem,
         scratch_shapes=bufs + [
             pltpu.VMEM((rows, 2 * SUB, LANES), jnp.float32),
@@ -407,9 +402,15 @@
             dma((CHUNKS * length,)), dma((CHUNKS * length,)),
             dma((windows * CHUNKS,)), dma((windows * CHUNKS,)),
             dma((windows,)), dma((windows,)),
+            pltpu.VMEM((1 + rows, 2 * SUB, LANES), jnp.bfloat16),
+            pltpu.VMEM((SUB * rows // CHUNKS, SLICES * 2 * LANES), jnp.float32),
+            pltpu.VMEM((SUB * rows // CHUNKS, 2 * LANES), jnp.float32),
+            pltpu.VMEM((SUB * 2 * SUB, LANES), jnp.float32),
+            pltpu.VMEM((2 * SUB, LANES), jnp.float32),
         ],
         compiler_params=pltpu.CompilerParams(collective_id=0, has_side_effects=True),
-    )(pair_blocks, window_decay, own, jnp.asarray(lag_table()))
+    )(pair_blocks, window_decay, waveforms, segment_mask, jnp.asarray(high), jnp.asarray(low), jnp.asarray(twist),
+      jnp.asarray(lag_table()))
     return stacked.reshape(1, stations, slots * stations, LAGS)
 
 

time: 43.5 us -> 39.3 us (0.903)
  Pallas kernels: 40.8 us -> 36.8 us
    pallas_call x1 -> x0, Pallas kernels: 4.87 us -> none  [body(): pl.pallas_call(functools.partial(spectrum_kernel, stations), name='spectr...]
    pallas_call x1, Pallas kernels: 35.9 us -> 36.8 us  [body(): pl.pallas_call(functools.partial(correlate_kernel, n, windows, stations,...]
where the time goes in v3:
time: 39.3 us; the launch traced here: 39.1 us
  Pallas kernels  36.8 us (94%)
  local copies, waits for them, and re-layouts  1.62 us (4%)
  between operations  0.66 us (2%)
    pallas_call x1, Pallas kernels, body(): pl.pallas_call(functools.partial(correlate_kernel, n, windows, stations,...  36.8 us
    unnamed x1, local copies, waits for them, and re-layouts  1.62 us

profile of v3, /device:TPU:0, one launch (start us, length us, event | category | flops | bytes accessed | tf_op | source)
XLA Modules:
  0.0 39.1 jit_solution(7493186078259039427)
XLA Ops:
  0.7 36.8 %correlate.1 = bf16[256,384]{1,0:T(8,128)(2,1)} custom-call(s32[1,4]{1,0:T(1,128)} %pair_ref.1, f32[1]{0:T(128)S(6)} %copy.10.decay_ref, bf16[1,8,8,4096]{3,2,1,0:T(8,128)(2,1)} %x_ref.1, s32[1,8,8]{2,1,0:T(8,128)} %mask_ref.1, bf16[1024,256]{1,0:T(8,128)(2,1)} %constant.8.clone.high_ref, bf16[1024,256]{1,0:T(8,128)(2,1)} %constant.9.clone.low_ref, ...), custom_call_target="tpu_custom_call" | custom-call | tf_op jit(solution)/shard_map/correlate/pallas_call | solution.py:384
  37.5 1.6 %copy.11 = bf16[1,8,32,384]{3,2,1,0:T(8,128)(2,1)} copy(bf16[1,8,32,384]{3,2,1,0:T(8,128)(2,1)} %bitcast.1) | data formatting | bytes 393216

commit v4 on v3

--- a/solution.py
+++ b/solution.py
@@ -255,10 +255,10 @@
             rate_later(d).start()
     for c in range(1, CHUNKS):
         transform(c)
-        if 1 <= c - 1 < ahead:
-            send_own(c - 1)
-    for c in range(CHUNKS):
         bufs[c][me] = own_ref[span(c)]
+        if c < ahead:
+            send_own(c)
+    bufs[0][me] = own_ref[span(0)]
     loc_ref[...] = own_ref[1:1 + stations * segments].astype(jnp.float32)
 
     def combine(c):

time: 39.3 us -> 39.5 us (level)
  no operation moved by 1% of the time
where the time goes in v4:
time: 39.5 us; the launch traced here: 39.3 us
  Pallas kernels  37 us (94%)
  local copies, waits for them, and re-layouts  1.62 us (4%)
  between operations  0.66 us (2%)
    pallas_call x1, Pallas kernels, body(): pl.pallas_call(functools.partial(correlate_kernel, n, windows, stations,...  37 us
    unnamed x1, local copies, waits for them, and re-layouts  1.62 us

profile of v4, /device:TPU:0, one launch (start us, length us, event | category | flops | bytes accessed | tf_op | source)
XLA Modules:
  0.0 39.3 jit_solution(12226246249815189410)
XLA Ops:
  0.7 37.0 %correlate.1 = bf16[256,384]{1,0:T(8,128)(2,1)} custom-call(s32[1,4]{1,0:T(1,128)} %pair_ref.1, f32[1]{0:T(128)S(6)} %copy.10.decay_ref, bf16[1,8,8,4096]{3,2,1,0:T(8,128)(2,1)} %x_ref.1, s32[1,8,8]{2,1,0:T(8,128)} %mask_ref.1, bf16[1024,256]{1,0:T(8,128)(2,1)} %constant.8.clone.high_ref, bf16[1024,256]{1,0:T(8,128)(2,1)} %constant.9.clone.low_ref, ...), custom_call_target="tpu_custom_call" | custom-call | tf_op jit(solution)/shard_map/correlate/pallas_call | solution.py:384
  37.7 1.6 %copy.11 = bf16[1,8,32,384]{3,2,1,0:T(8,128)(2,1)} copy(bf16[1,8,32,384]{3,2,1,0:T(8,128)(2,1)} %bitcast.1) | data formatting | bytes 393216
